TPU v7x, 32 devices: a whole 2x2x4 slice. The times are simulated.
32 devices in a mesh: strip: 8 (over y, x, core), dom: 4 (over z).
Axes of the slice: x: 2, y: 2, z: 4, core: 2. Of those that a mesh axis runs over, the one named last changes fastest.
Arguments:
- rhs: float32 [32, 8, 64, 512], P('strip', None, None, 'dom'), may hold values from -6 to 6
- diag_inv: bfloat16 [32, 64, 64, 512], P('strip', None, None, 'dom'), may hold values from -0.75 to 0.75
- lower_blocks: bfloat16 [24, 2, 64, 64, 512], P('strip', None, None, None, 'dom'), may hold values from -0.4375 to 0.4375
- lower_index: int32 [24, 2, 512], P('strip', None, 'dom'), may hold values from 0 to 127
- upper_blocks: bfloat16 [24, 2, 64, 64, 512], P('strip', None, None, None, 'dom'), may hold values from -0.4375 to 0.4375
- upper_index: int32 [24, 2, 512], P('strip', None, 'dom'), may hold values from 0 to 127
- cross_lower: bfloat16 [8, 2, 64, 64, 512], P('strip', None, None, None, 'dom'), may hold values from -0.4375 to 0.4375
- cross_lower_index: int32 [8, 2, 512], P('strip', None, 'dom'), may hold values from 0 to 383
- cross_upper: bfloat16 [8, 2, 64, 64, 512], P('strip', None, None, None, 'dom'), may hold values from -0.4375 to 0.4375
- cross_upper_index: int32 [8, 2, 512], P('strip', None, 'dom'), may hold values from 0 to 383
Outputs:
- result: float32 [32, 8, 64, 512], P('strip', None, None, 'dom')
Inputs may be any that keep to these rules, and one draw needn't show every extreme that they name: `lower_index`: block indices within one partition's level. `upper_index`: block indices within one partition's level. `cross_lower_index`: indices over the three partitions p - 1, p, p + 1 of the neighbouring strip's interface. `cross_upper_index`: indices over the three partitions p - 1, p, p + 1 of the neighbouring strip's interface.
All inputs are finite; a program needn't handle non-finite values.
Results may differ from a plain program's by a relative error of at most 0.0003.
Values sent between devices are 32-bit elements; how exact they have to be, the bound alone decides.
No kernel may reach another device: no remote copies, remote signals or barrier semaphores. Data moves between devices by JAX's collectives and lax.ppermute only.
A program may use at most 128 MiB of HBM per device.

v0:
```python
import jax
import jax.numpy as jnp
from jax import lax
from jax.sharding import PartitionSpec as P


def with_halo(x, sides, width):
    for axis, dim in sides:
        size, length = (lax.axis_size(axis), x.shape[dim])
        up = [(i, (i + 1) % size) for i in range(size - 1)]
        down = [(j, i) for i, j in up]
        last = lax.slice_in_dim(x, length - width, length, axis=dim)
        first = lax.slice_in_dim(x, 0, width, axis=dim)
        before = lax.ppermute(last, axis, up)
        after = lax.ppermute(first, axis, down)
        x = jnp.concatenate([before, x, after], axis=dim)
    return x


def passed_along(block, axis, distance):
    devices = range(lax.axis_size(axis))
    route = [(i - distance, i) for i in devices if i - distance in devices]
    return lax.ppermute(block, axis, route)


def apply_block(blocks, vector):
    return jnp.einsum(
        "abc,rbc->rac", blocks.astype(jnp.float32), vector, precision=lax.Precision.HIGHEST
    )


def neighbour_terms(blocks, indices, vector):
    total = apply_block(blocks[0], jnp.take(vector, indices[0], axis=2))
    total = total + apply_block(blocks[1], jnp.take(vector, indices[1], axis=2))
    return total


def on_device(
    rhs,
    diag_inv,
    lower_blocks,
    lower_index,
    upper_blocks,
    upper_index,
    cross_lower,
    cross_lower_index,
    cross_upper,
    cross_upper_index,
):
    levels = rhs.shape[0]
    block_count = rhs.shape[3]
    forward = []
    for level_no in range(levels - 1):
        total = rhs[level_no]
        if level_no > 0:
            total = total - neighbour_terms(
                lower_blocks[level_no - 1], lower_index[level_no - 1], forward[level_no - 1]
            )
        forward.append(apply_block(diag_inv[level_no], total))
    local_part = rhs[levels - 1] - neighbour_terms(
        lower_blocks[levels - 2], lower_index[levels - 2], forward[levels - 2]
    )
    strip_count = lax.axis_size("strip")

    def fetch_prior(current):
        extended = with_halo(current, (("dom", 2),), block_count)
        return passed_along(extended, "strip", 1)

    def fetch_later(current):
        extended = with_halo(current, (("dom", 2),), block_count)
        return passed_along(extended, "strip", -1)

    def forward_turn(turn_no, current):
        padded = fetch_prior(current)
        total = local_part - neighbour_terms(cross_lower[0], cross_lower_index[0], padded)
        return apply_block(diag_inv[levels - 1], total)

    interface = lax.fori_loop(0, strip_count, forward_turn, jnp.zeros_like(local_part))

    def backward_turn(turn_no, current):
        padded = fetch_later(current)
        total = neighbour_terms(cross_upper[0], cross_upper_index[0], padded)
        return interface - apply_block(diag_inv[levels - 1], total)

    swept = lax.fori_loop(0, strip_count, backward_turn, jnp.zeros_like(interface))
    result = [None] * levels
    result[levels - 1] = swept
    for level_no in range(levels - 2, -1, -1):
        total = neighbour_terms(upper_blocks[level_no], upper_index[level_no], result[level_no + 1])
        result[level_no] = forward[level_no] - apply_block(diag_inv[level_no], total)
    return jnp.stack(result)


def solution(mesh):
    in_specs = (
        P("strip", None, None, "dom"),
        P("strip", None, None, "dom"),
        P("strip", None, None, None, "dom"),
        P("strip", None, "dom"),
        P("strip", None, None, None, "dom"),
        P("strip", None, "dom"),
        P("strip", None, None, None, "dom"),
        P("strip", None, "dom"),
        P("strip", None, None, None, "dom"),
        P("strip", None, "dom"),
    )
    out_specs = P("strip", None, None, "dom")
    return jax.shard_map(
        on_device, mesh=mesh, in_specs=in_specs, out_specs=out_specs, check_vma=False
    )
```

profile of v0, /device:TPU:27, one launch (start us, length us, event | category | flops | bytes accessed | tf_op | source)
XLA Modules:
  0.0 864.8 jit_solution(5750053470409176384)
XLA Ops:
  0.8 13.1 %copy.48 = bf16[4,64,64,128]{2,1,3,0:T(8,128)(2,1)} copy(bf16[4,64,64,128]{3,2,1,0:T(8,128)(2,1)} %param.19) | data formatting | bytes 8388608 | tf_op args[1]
  21.6 6.0 fusion.209
  98.4 7.4 copy.60
  105.9 335.2 %while.21 = (s32[]{:T(128)}, f32[8,64,128]{1,0,2:T(8,128)S(1)}, s32[1,2,128]{2,1,0:T(2,128)S(1)}, bf16[1,2,64,64,128]{3,2,4,1,0:T(8,128)(2,1)}, f32[8,64,128]{1,...) while((s32[]{:T(128)}, f32[8,64,128]{1,0,2:T(8,128)S(1)}, s32[1,2,128]{2,1,0:T(2,128)S(1)}, ...), condition=%wide.region_1.4_spmd, body=%wide.region_0.3_spmd.sunk | while | flops 151653888 | bytes 18363076 | solution.py:78
  121.9 8.9 %collective-permute-done.2 = f32[8,64,384]{2,1,0:T(8,128)S(1)} collective-permute-done((f32[8,64,384]{2,1,0:T(8,128)S(1)}, f32[8,64,384]{2,1,0:T(8,128)S(1)}, u32[]{:S(2)}, u32[]{:S(2)}) %collective-permute-start.2) | collective-permute-done | bytes 786464 | tf_op jit(solution)/shard_map/while/body/eval_jaxpr/ppermute | solution.py:23
  137.9 5.0 fusion.243
  158.3 5.7 collective-permute-start.2
  164.1 8.9 %collective-permute-done.2 = f32[8,64,384]{2,1,0:T(8,128)S(1)} collective-permute-done((f32[8,64,384]{2,1,0:T(8,128)S(1)}, f32[8,64,384]{2,1,0:T(8,128)S(1)}, u32[]{:S(2)}, u32[]{:S(2)}) %collective-permute-start.2) | collective-permute-done | bytes 786464 | tf_op jit(solution)/shard_map/while/body/eval_jaxpr/ppermute | solution.py:23
  180.1 5.0 fusion.243
  200.7 5.5 collective-permute-start.2
  206.3 8.9 %collective-permute-done.2 = f32[8,64,384]{2,1,0:T(8,128)S(1)} collective-permute-done((f32[8,64,384]{2,1,0:T(8,128)S(1)}, f32[8,64,384]{2,1,0:T(8,128)S(1)}, u32[]{:S(2)}, u32[]{:S(2)}) %collective-permute-start.2) | collective-permute-done | bytes 786464 | tf_op jit(solution)/shard_map/while/body/eval_jaxpr/ppermute | solution.py:23
  222.3 5.0 fusion.243
  242.3 5.7 collective-permute-start.2
  248.1 8.9 %collective-permute-done.2 = f32[8,64,384]{2,1,0:T(8,128)S(1)} collective-permute-done((f32[8,64,384]{2,1,0:T(8,128)S(1)}, f32[8,64,384]{2,1,0:T(8,128)S(1)}, u32[]{:S(2)}, u32[]{:S(2)}) %collective-permute-start.2) | collective-permute-done | bytes 786464 | tf_op jit(solution)/shard_map/while/body/eval_jaxpr/ppermute | solution.py:23
  264.1 5.0 fusion.243
  284.0 5.8 collective-permute-start.2
  289.9 8.9 %collective-permute-done.2 = f32[8,64,384]{2,1,0:T(8,128)S(1)} collective-permute-done((f32[8,64,384]{2,1,0:T(8,128)S(1)}, f32[8,64,384]{2,1,0:T(8,128)S(1)}, u32[]{:S(2)}, u32[]{:S(2)}) %collective-permute-start.2) | collective-permute-done | bytes 786464 | tf_op jit(solution)/shard_map/while/body/eval_jaxpr/ppermute | solution.py:23
  305.9 5.0 fusion.243
  325.8 5.8 collective-permute-start.2
  331.6 8.9 %collective-permute-done.2 = f32[8,64,384]{2,1,0:T(8,128)S(1)} collective-permute-done((f32[8,64,384]{2,1,0:T(8,128)S(1)}, f32[8,64,384]{2,1,0:T(8,128)S(1)}, u32[]{:S(2)}, u32[]{:S(2)}) %collective-permute-start.2) | collective-permute-done | bytes 786464 | tf_op jit(solution)/shard_map/while/body/eval_jaxpr/ppermute | solution.py:23
  347.6 5.0 fusion.243
  367.5 5.8 collective-permute-start.2
  373.4 8.9 %collective-permute-done.2 = f32[8,64,384]{2,1,0:T(8,128)S(1)} collective-permute-done((f32[8,64,384]{2,1,0:T(8,128)S(1)}, f32[8,64,384]{2,1,0:T(8,128)S(1)}, u32[]{:S(2)}, u32[]{:S(2)}) %collective-permute-start.2) | collective-permute-done | bytes 786464 | tf_op jit(solution)/shard_map/while/body/eval_jaxpr/ppermute | solution.py:23
  389.4 5.0 fusion.243
  409.3 5.8 collective-permute-start.2
  415.1 8.9 %collective-permute-done.2 = f32[8,64,384]{2,1,0:T(8,128)S(1)} collective-permute-done((f32[8,64,384]{2,1,0:T(8,128)S(1)}, f32[8,64,384]{2,1,0:T(8,128)S(1)}, u32[]{:S(2)}, u32[]{:S(2)}) %collective-permute-start.2) | collective-permute-done | bytes 786464 | tf_op jit(solution)/shard_map/while/body/eval_jaxpr/ppermute | solution.py:23
  431.1 5.0 fusion.243
  441.1 7.8 copy.62
  448.9 329.3 %while.22 = (s32[]{:T(128)}, f32[8,64,128]{1,0,2:T(8,128)S(1)}, s32[1,2,128]{2,1,0:T(2,128)S(1)}, bf16[1,2,64,64,128]{3,2,4,1,0:T(8,128)(2,1)}, bf16[4,64,64,128...) while((s32[]{:T(128)}, f32[8,64,128]{1,0,2:T(8,128)S(1)}, ...), condition=%wide.region_3.6_spmd.clone, body=%wide.region_2.5_spmd.clone.sunk | while | flops 151719424 | bytes 18887384 | solution.py:85
  463.4 10.9 %collective-permute-done.5 = f32[8,64,384]{2,1,0:T(8,128)S(1)} collective-permute-done((f32[8,64,384]{2,1,0:T(8,128)S(1)}, f32[8,64,384]{2,1,0:T(8,128)S(1)}, u32[]{:S(2)}, u32[]{:S(2)}) %collective-permute-start.5) | collective-permute-done | bytes 786464 | tf_op jit(solution)/shard_map/while/body/eval_jaxpr/ppermute | solution.py:23
  481.5 5.0 fusion.252
  505.1 12.0 %collective-permute-done.5 = f32[8,64,384]{2,1,0:T(8,128)S(1)} collective-permute-done((f32[8,64,384]{2,1,0:T(8,128)S(1)}, f32[8,64,384]{2,1,0:T(8,128)S(1)}, u32[]{:S(2)}, u32[]{:S(2)}) %collective-permute-start.5) | collective-permute-done | bytes 786464 | tf_op jit(solution)/shard_map/while/body/eval_jaxpr/ppermute | solution.py:23
  524.2 5.0 fusion.252
  545.9 12.2 %collective-permute-done.5 = f32[8,64,384]{2,1,0:T(8,128)S(1)} collective-permute-done((f32[8,64,384]{2,1,0:T(8,128)S(1)}, f32[8,64,384]{2,1,0:T(8,128)S(1)}, u32[]{:S(2)}, u32[]{:S(2)}) %collective-permute-start.5) | collective-permute-done | bytes 786464 | tf_op jit(solution)/shard_map/while/body/eval_jaxpr/ppermute | solution.py:23
  565.3 5.0 fusion.252
  586.3 12.2 %collective-permute-done.5 = f32[8,64,384]{2,1,0:T(8,128)S(1)} collective-permute-done((f32[8,64,384]{2,1,0:T(8,128)S(1)}, f32[8,64,384]{2,1,0:T(8,128)S(1)}, u32[]{:S(2)}, u32[]{:S(2)}) %collective-permute-start.5) | collective-permute-done | bytes 786464 | tf_op jit(solution)/shard_map/while/body/eval_jaxpr/ppermute | solution.py:23
  605.6 5.0 fusion.252
  626.9 12.2 %collective-permute-done.5 = f32[8,64,384]{2,1,0:T(8,128)S(1)} collective-permute-done((f32[8,64,384]{2,1,0:T(8,128)S(1)}, f32[8,64,384]{2,1,0:T(8,128)S(1)}, u32[]{:S(2)}, u32[]{:S(2)}) %collective-permute-start.5) | collective-permute-done | bytes 786464 | tf_op jit(solution)/shard_map/while/body/eval_jaxpr/ppermute | solution.py:23
  646.3 5.0 fusion.252
  667.6 12.2 %collective-permute-done.5 = f32[8,64,384]{2,1,0:T(8,128)S(1)} collective-permute-done((f32[8,64,384]{2,1,0:T(8,128)S(1)}, f32[8,64,384]{2,1,0:T(8,128)S(1)}, u32[]{:S(2)}, u32[]{:S(2)}) %collective-permute-start.5) | collective-permute-done | bytes 786464 | tf_op jit(solution)/shard_map/while/body/eval_jaxpr/ppermute | solution.py:23
  686.9 5.0 fusion.252
  708.2 12.2 %collective-permute-done.5 = f32[8,64,384]{2,1,0:T(8,128)S(1)} collective-permute-done((f32[8,64,384]{2,1,0:T(8,128)S(1)}, f32[8,64,384]{2,1,0:T(8,128)S(1)}, u32[]{:S(2)}, u32[]{:S(2)}) %collective-permute-start.5) | collective-permute-done | bytes 786464 | tf_op jit(solution)/shard_map/while/body/eval_jaxpr/ppermute | solution.py:23
  727.6 5.0 fusion.252
  748.9 12.2 %collective-permute-done.5 = f32[8,64,384]{2,1,0:T(8,128)S(1)} collective-permute-done((f32[8,64,384]{2,1,0:T(8,128)S(1)}, f32[8,64,384]{2,1,0:T(8,128)S(1)}, u32[]{:S(2)}, u32[]{:S(2)}) %collective-permute-start.5) | collective-permute-done | bytes 786464 | tf_op jit(solution)/shard_map/while/body/eval_jaxpr/ppermute | solution.py:23
  768.2 5.0 fusion.252
  779.8 6.0 fusion.208
  815.1 5.3 fusion.66
  841.2 5.3 fusion.62
  (306 shorter events, 524.1 us)
Async XLA Ops:
  106.1 7.1 collective-permute-start
  108.2 8.8 %collective-permute-start.1 = (f32[8,64,128]{2,1,0:T(8,128)S(1)}, f32[8,64,128]{2,1,0:T(8,128)S(1)}, u32[]{:S(2)}, u32[]{:S(2)}) collective-permute-start(f32[8,64,128]{2,1,0:T(8,128)S(1)} %copy.91), channel_id=1, source_target_pairs={{0,1},{1,2},{2,3},{4,5},{5,6},{6,7},{8,9},{9,10},{10,11},{12,13},{... | collective-permute-start | bytes 786440 | tf_op jit(solution)/shard_map/while/body/eval_jaxpr/ppermute | solution.py:14
  117.1 13.7 %collective-permute-start.2 = (f32[8,64,384]{2,1,0:T(8,128)S(1)}, f32[8,64,384]{2,1,0:T(8,128)S(1)}, u32[]{:S(2)}, u32[]{:S(2)}) collective-permute-start(f32[8,64,384]{2,1,0:T(8,128)S(1)} %pad_maximum_fusion.5), channel_id=1, source_target_pairs={{0,4},{4,8},{8,12},{12,16},{16,20},{20,24},{24,28},{1,5},{5,9},{9,... | collective-permute-start | bytes 2359304 | tf_op jit(solution)/shard_map/while/body/eval_jaxpr/ppermute | solution.py:23
  148.1 6.3 collective-permute-start
  150.2 8.1 collective-permute-start.1
  158.3 14.7 %collective-permute-start.2 = (f32[8,64,384]{2,1,0:T(8,128)S(1)}, f32[8,64,384]{2,1,0:T(8,128)S(1)}, u32[]{:S(2)}, u32[]{:S(2)}) collective-permute-start(f32[8,64,384]{2,1,0:T(8,128)S(1)} %pad_maximum_fusion.5), channel_id=1, source_target_pairs={{0,4},{4,8},{8,12},{12,16},{16,20},{20,24},{24,28},{1,5},{5,9},{9,... | collective-permute-start | bytes 2359304 | tf_op jit(solution)/shard_map/while/body/eval_jaxpr/ppermute | solution.py:23
  190.3 6.5 collective-permute-start
  192.4 8.3 collective-permute-start.1
  200.7 14.4 %collective-permute-start.2 = (f32[8,64,384]{2,1,0:T(8,128)S(1)}, f32[8,64,384]{2,1,0:T(8,128)S(1)}, u32[]{:S(2)}, u32[]{:S(2)}) collective-permute-start(f32[8,64,384]{2,1,0:T(8,128)S(1)} %pad_maximum_fusion.5), channel_id=1, source_target_pairs={{0,4},{4,8},{8,12},{12,16},{16,20},{20,24},{24,28},{1,5},{5,9},{9,... | collective-permute-start | bytes 2359304 | tf_op jit(solution)/shard_map/while/body/eval_jaxpr/ppermute | solution.py:23
  232.5 6.0 collective-permute-start
  234.2 8.1 collective-permute-start.1
  242.3 14.7 %collective-permute-start.2 = (f32[8,64,384]{2,1,0:T(8,128)S(1)}, f32[8,64,384]{2,1,0:T(8,128)S(1)}, u32[]{:S(2)}, u32[]{:S(2)}) collective-permute-start(f32[8,64,384]{2,1,0:T(8,128)S(1)} %pad_maximum_fusion.5), channel_id=1, source_target_pairs={{0,4},{4,8},{8,12},{12,16},{16,20},{20,24},{24,28},{1,5},{5,9},{9,... | collective-permute-start | bytes 2359304 | tf_op jit(solution)/shard_map/while/body/eval_jaxpr/ppermute | solution.py:23
  274.3 5.8 collective-permute-start
  275.9 8.0 collective-permute-start.1
  284.0 14.7 %collective-permute-start.2 = (f32[8,64,384]{2,1,0:T(8,128)S(1)}, f32[8,64,384]{2,1,0:T(8,128)S(1)}, u32[]{:S(2)}, u32[]{:S(2)}) collective-permute-start(f32[8,64,384]{2,1,0:T(8,128)S(1)} %pad_maximum_fusion.5), channel_id=1, source_target_pairs={{0,4},{4,8},{8,12},{12,16},{16,20},{20,24},{24,28},{1,5},{5,9},{9,... | collective-permute-start | bytes 2359304 | tf_op jit(solution)/shard_map/while/body/eval_jaxpr/ppermute | solution.py:23
  316.0 5.8 collective-permute-start
  317.7 8.0 collective-permute-start.1
  325.8 14.7 %collective-permute-start.2 = (f32[8,64,384]{2,1,0:T(8,128)S(1)}, f32[8,64,384]{2,1,0:T(8,128)S(1)}, u32[]{:S(2)}, u32[]{:S(2)}) collective-permute-start(f32[8,64,384]{2,1,0:T(8,128)S(1)} %pad_maximum_fusion.5), channel_id=1, source_target_pairs={{0,4},{4,8},{8,12},{12,16},{16,20},{20,24},{24,28},{1,5},{5,9},{9,... | collective-permute-start | bytes 2359304 | tf_op jit(solution)/shard_map/while/body/eval_jaxpr/ppermute | solution.py:23
  357.8 5.8 collective-permute-start
  359.4 8.0 collective-permute-start.1
  367.5 14.7 %collective-permute-start.2 = (f32[8,64,384]{2,1,0:T(8,128)S(1)}, f32[8,64,384]{2,1,0:T(8,128)S(1)}, u32[]{:S(2)}, u32[]{:S(2)}) collective-permute-start(f32[8,64,384]{2,1,0:T(8,128)S(1)} %pad_maximum_fusion.5), channel_id=1, source_target_pairs={{0,4},{4,8},{8,12},{12,16},{16,20},{20,24},{24,28},{1,5},{5,9},{9,... | collective-permute-start | bytes 2359304 | tf_op jit(solution)/shard_map/while/body/eval_jaxpr/ppermute | solution.py:23
  399.5 5.8 collective-permute-start
  401.2 8.0 collective-permute-start.1
  409.3 14.7 %collective-permute-start.2 = (f32[8,64,384]{2,1,0:T(8,128)S(1)}, f32[8,64,384]{2,1,0:T(8,128)S(1)}, u32[]{:S(2)}, u32[]{:S(2)}) collective-permute-start(f32[8,64,384]{2,1,0:T(8,128)S(1)} %pad_maximum_fusion.5), channel_id=1, source_target_pairs={{0,4},{4,8},{8,12},{12,16},{16,20},{20,24},{24,28},{1,5},{5,9},{9,... | collective-permute-start | bytes 2359304 | tf_op jit(solution)/shard_map/while/body/eval_jaxpr/ppermute | solution.py:23
  449.1 5.8 collective-permute-start.3
  450.8 8.0 collective-permute-start.4
  458.9 15.5 %collective-permute-start.5 = (f32[8,64,384]{2,1,0:T(8,128)S(1)}, f32[8,64,384]{2,1,0:T(8,128)S(1)}, u32[]{:S(2)}, u32[]{:S(2)}) collective-permute-start(f32[8,64,384]{2,1,0:T(8,128)S(1)} %pad_maximum_fusion.6), channel_id=1, source_target_pairs={{4,0},{8,4},{12,8},{16,12},{20,16},{24,20},{28,24},{5,1},{9,5},{13... | collective-permute-start | bytes 2359304 | tf_op jit(solution)/shard_map/while/body/eval_jaxpr/ppermute | solution.py:23
  491.7 7.0 collective-permute-start.3
  493.3 9.5 %collective-permute-start.4 = (f32[8,64,128]{2,1,0:T(8,128)S(1)}, f32[8,64,128]{2,1,0:T(8,128)S(1)}, u32[]{:S(2)}, u32[]{:S(2)}) collective-permute-start(f32[8,64,128]{2,1,0:T(8,128)S(1)} %broadcast_select_fusion.2), channel_id=1, source_target_pairs={{0,1},{1,2},{2,3},{4,5},{5,6},{6,7},{8,9},{9,10},{10,11},{12,13},{... | collective-permute-start | bytes 786440 | tf_op jit(solution)/shard_map/while/body/eval_jaxpr/ppermute | solution.py:14
  502.9 14.2 %collective-permute-start.5 = (f32[8,64,384]{2,1,0:T(8,128)S(1)}, f32[8,64,384]{2,1,0:T(8,128)S(1)}, u32[]{:S(2)}, u32[]{:S(2)}) collective-permute-start(f32[8,64,384]{2,1,0:T(8,128)S(1)} %pad_maximum_fusion.6), channel_id=1, source_target_pairs={{4,0},{8,4},{12,8},{16,12},{20,16},{24,20},{28,24},{5,1},{9,5},{13... | collective-permute-start | bytes 2359304 | tf_op jit(solution)/shard_map/while/body/eval_jaxpr/ppermute | solution.py:23
  534.4 5.4 collective-permute-start.3
  536.1 7.8 collective-permute-start.4
  544.0 14.2 %collective-permute-start.5 = (f32[8,64,384]{2,1,0:T(8,128)S(1)}, f32[8,64,384]{2,1,0:T(8,128)S(1)}, u32[]{:S(2)}, u32[]{:S(2)}) collective-permute-start(f32[8,64,384]{2,1,0:T(8,128)S(1)} %pad_maximum_fusion.6), channel_id=1, source_target_pairs={{4,0},{8,4},{12,8},{16,12},{20,16},{24,20},{28,24},{5,1},{9,5},{13... | collective-permute-start | bytes 2359304 | tf_op jit(solution)/shard_map/while/body/eval_jaxpr/ppermute | solution.py:23
  575.5 4.9 collective-permute-start.3
  577.1 7.1 collective-permute-start.4
  584.3 14.2 %collective-permute-start.5 = (f32[8,64,384]{2,1,0:T(8,128)S(1)}, f32[8,64,384]{2,1,0:T(8,128)S(1)}, u32[]{:S(2)}, u32[]{:S(2)}) collective-permute-start(f32[8,64,384]{2,1,0:T(8,128)S(1)} %pad_maximum_fusion.6), channel_id=1, source_target_pairs={{4,0},{8,4},{12,8},{16,12},{20,16},{24,20},{28,24},{5,1},{9,5},{13... | collective-permute-start | bytes 2359304 | tf_op jit(solution)/shard_map/while/body/eval_jaxpr/ppermute | solution.py:23
  615.9 5.2 collective-permute-start.3
  617.8 7.1 collective-permute-start.4
  625.0 14.2 %collective-permute-start.5 = (f32[8,64,384]{2,1,0:T(8,128)S(1)}, f32[8,64,384]{2,1,0:T(8,128)S(1)}, u32[]{:S(2)}, u32[]{:S(2)}) collective-permute-start(f32[8,64,384]{2,1,0:T(8,128)S(1)} %pad_maximum_fusion.6), channel_id=1, source_target_pairs={{4,0},{8,4},{12,8},{16,12},{20,16},{24,20},{28,24},{5,1},{9,5},{13... | collective-permute-start | bytes 2359304 | tf_op jit(solution)/shard_map/while/body/eval_jaxpr/ppermute | solution.py:23
  656.5 5.2 collective-permute-start.3
  658.4 7.1 collective-permute-start.4
  665.6 14.2 %collective-permute-start.5 = (f32[8,64,384]{2,1,0:T(8,128)S(1)}, f32[8,64,384]{2,1,0:T(8,128)S(1)}, u32[]{:S(2)}, u32[]{:S(2)}) collective-permute-start(f32[8,64,384]{2,1,0:T(8,128)S(1)} %pad_maximum_fusion.6), channel_id=1, source_target_pairs={{4,0},{8,4},{12,8},{16,12},{20,16},{24,20},{28,24},{5,1},{9,5},{13... | collective-permute-start | bytes 2359304 | tf_op jit(solution)/shard_map/while/body/eval_jaxpr/ppermute | solution.py:23
  697.2 5.2 collective-permute-start.3
  699.1 7.1 collective-permute-start.4
  706.3 14.2 %collective-permute-start.5 = (f32[8,64,384]{2,1,0:T(8,128)S(1)}, f32[8,64,384]{2,1,0:T(8,128)S(1)}, u32[]{:S(2)}, u32[]{:S(2)}) collective-permute-start(f32[8,64,384]{2,1,0:T(8,128)S(1)} %pad_maximum_fusion.6), channel_id=1, source_target_pairs={{4,0},{8,4},{12,8},{16,12},{20,16},{24,20},{28,24},{5,1},{9,5},{13... | collective-permute-start | bytes 2359304 | tf_op jit(solution)/shard_map/while/body/eval_jaxpr/ppermute | solution.py:23
  737.8 5.2 collective-permute-start.3
  739.7 7.1 collective-permute-start.4
  746.9 14.2 %collective-permute-start.5 = (f32[8,64,384]{2,1,0:T(8,128)S(1)}, f32[8,64,384]{2,1,0:T(8,128)S(1)}, u32[]{:S(2)}, u32[]{:S(2)}) collective-permute-start(f32[8,64,384]{2,1,0:T(8,128)S(1)} %pad_maximum_fusion.6), channel_id=1, source_target_pairs={{4,0},{8,4},{12,8},{16,12},{20,16},{24,20},{28,24},{5,1},{9,5},{13... | collective-permute-start | bytes 2359304 | tf_op jit(solution)/shard_map/while/body/eval_jaxpr/ppermute | solution.py:23
  (12 other events, 413.2 us)
where the time goes:
time: 876 us; the launch traced here: 865 us
  matrix products  324 us (37%)
  waiting for transfers between devices  273 us (31%)
  local copies, waits for them, and re-layouts  150 us (17%)
  starting transfers between devices  113 us (13%)
    dot_general x66, matrix products, apply_block(): jnp.einsum('abc,rbc->rac', blocks.astype(jnp.float32), vector, precision=...  324 us
    ppermute x16, waiting for transfers between devices, passed_along(): return lax.ppermute(block, axis, route)  167 us
    unnamed x42, local copies, waits for them, and re-layouts  72.5 us
    ppermute x16, starting transfers between devices, passed_along(): return lax.ppermute(block, axis, route)  63.2 us
    ppermute x16, waiting for transfers between devices, with_halo(): before = lax.ppermute(last, axis, up)  62 us
    ppermute x16, waiting for transfers between devices, with_halo(): after = lax.ppermute(first, axis, down)  43.5 us
    ppermute x16, starting transfers between devices, with_halo(): after = lax.ppermute(first, axis, down)  28.8 us
    gather x22, local copies, waits for them, and re-layouts, neighbour_terms(): total = apply_block(blocks[0], jnp.take(vector, indices[0], axis=2))  22.5 us
  transfers between devices with their start and end apart: 48, of which 48 were waited for; matrix products, arithmetic and copies ran while one was open for 0% of the time, Pallas kernels for 0%

commit v1 on v0

v1 whole, which is shorter than its diff:
```python
import functools

import jax
import jax.numpy as jnp
from jax import lax
from jax.experimental import pallas as pl
from jax.experimental.pallas import tpu as pltpu
from jax.sharding import PartitionSpec as P

WAVES = 2
SPACING = 2
SUB = 8
ANY = pl.BlockSpec(memory_space=pl.ANY)
VMEM = pl.BlockSpec(memory_space=pltpu.VMEM)
SMEM = pl.BlockSpec(memory_space=pltpu.SMEM)
F32 = jnp.float32


def transposed_sum(rows):
    sub = lax.broadcasted_iota(jnp.int32, rows[0].shape, 0)
    shift = 1
    while len(rows) > 1:
        keep = (sub & shift) == 0
        rows = [
            jnp.where(keep, a, b) + pltpu.roll(jnp.where(keep, b, a), shift, 0)
            for a, b in zip(rows[0::2], rows[1::2])
        ]
        shift *= 2
    return rows[0]


def block_product(pairs, sides, emit):
    size = pairs[0][0].shape[0]

    def group(group_no, carry):
        first = pl.multiple_of(group_no * SUB, SUB)
        partial = [[] for _ in range(sides)]
        for i in range(SUB):
            sums = [None] * sides
            for blocks, vector in pairs:
                row = blocks[first + i].astype(F32)
                for b in range(0, size, SUB):
                    piece = row[b : b + SUB]
                    for side in range(sides):
                        term = piece * vector[side, b : b + SUB]
                        sums[side] = term if sums[side] is None else sums[side] + term
            for side in range(sides):
                partial[side].append(sums[side])
        for side in range(sides):
            emit(side, first, transposed_sum(partial[side]))
        return carry

    lax.fori_loop(0, size // SUB, group, 0)


def take_lanes(values, index):
    return jnp.take_along_axis(values, index, axis=1, mode="promise_in_bounds")


def take_blocks(target, source, index_row):
    sides, size, count = source.shape
    index = jnp.broadcast_to(index_row, (size, count))
    for side in range(sides):
        target[side] = take_lanes(source[side], index)


def take_wide(target, straight, pair, odd, parity, index_row):
    sides, size, count = straight.shape
    index = jnp.broadcast_to(index_row, (size, count))
    part = (index >= count).astype(jnp.int32) + (index >= 2 * count).astype(jnp.int32)
    index = index - part * count
    own = part == 1
    from_pair = part == 2 - 2 * parity
    for side in range(sides):
        value = jnp.where(from_pair, take_lanes(pair[side], index), take_lanes(odd[side], index))
        target[side] = jnp.where(own, take_lanes(straight[side], index), value)


def start_all(copies):
    for copy in copies:
        copy.start()


def interior_forward(first, flag, rhs, diag, lower, index, *refs):
    z, local, start, rhs_v, diag_v, lower_v, gathered, total, sem = refs[-9:]
    sides = local.shape[0]
    levels = diag_v.shape[0]

    @pl.when(flag[0] != 0)
    def _():
        rhs_copy = pltpu.make_async_copy(rhs.at[:, pl.ds(first, sides)], rhs_v, sem.at[0])
        diag_copy = [pltpu.make_async_copy(diag.at[n], diag_v.at[n], sem.at[1 + n]) for n in range(levels)]
        lower_copy = [
            pltpu.make_async_copy(lower.at[n], lower_v.at[n], sem.at[1 + levels + n]) for n in range(levels - 1)
        ]
        rhs_copy.start()
        diag_copy[0].start()
        for n in range(levels - 1):
            lower_copy[n].start()
            diag_copy[n + 1].start()
        rhs_copy.wait()
        diag_copy[0].wait()

        def put(target):
            def emit(side, row, value):
                target[side, pl.ds(row, SUB)] = value

            return emit

        block_product([(diag_v.at[0], rhs_v.at[0])], sides, put(z.at[0]))
        for n in range(1, levels):
            lower_copy[n - 1].wait()
            for k in range(2):
                take_blocks(gathered.at[k], z.at[n - 1], index[n - 1, k][None])
            goal = local if n == levels - 1 else total

            def rest(side, row, value, n=n, goal=goal):
                goal[side, pl.ds(row, SUB)] = rhs_v[n, side, pl.ds(row, SUB)] - value

            block_product([(lower_v.at[n - 1, k], gathered.at[k]) for k in range(2)], sides, rest)
            diag_copy[n].wait()
            block_product([(diag_v.at[n], goal)], sides, put(start if n == levels - 1 else z.at[n]))


def run_interior_forward(first, flag, rhs, diag, lower, index, sides, earlier=None):
    levels, _, size, count = rhs.shape
    shapes = [(levels - 1, sides, size, count), (sides, size, count), (sides, size, count)]
    return pl.pallas_call(
        functools.partial(interior_forward, first),
        out_shape=[jax.ShapeDtypeStruct(s, F32) for s in shapes],
        in_specs=[SMEM, ANY, ANY, ANY, VMEM] + [VMEM if earlier is None else ANY] * (0 if earlier is None else 3),
        out_specs=[VMEM] * 3,
        scratch_shapes=[
            pltpu.VMEM((levels, sides, size, count), F32),
            pltpu.VMEM(diag.shape, diag.dtype),
            pltpu.VMEM(lower.shape, lower.dtype),
            pltpu.VMEM((2, sides, size, count), F32),
            pltpu.VMEM((sides, size, count), F32),
            pltpu.SemaphoreType.DMA((2 * levels,)),
        ],
        name="interior_forward",
    )(flag, rhs, diag, lower, index, *(earlier or ()))


def interface_step(flags, index, base, straight, pair, odd, held, cross, diag, out, cross_v, diag_v, gathered, total, sem, *, backward):
    sides = base.shape[0]

    @pl.when(flags[0] != 0)
    def _():
        copies = [pltpu.make_async_copy(cross.at[0, k], cross_v.at[k], sem.at[k]) for k in range(2)]
        copies.append(pltpu.make_async_copy(diag.at[diag.shape[0] - 1], diag_v, sem.at[2]))
        start_all(copies)
        for k in range(2):
            take_wide(gathered.at[k], straight, pair, odd, flags[1], index[0, k][None])

        def middle(side, row, value):
            if backward:
                total[side, pl.ds(row, SUB)] = value
            else:
                total[side, pl.ds(row, SUB)] = base[side, pl.ds(row, SUB)] - value

        def last(side, row, value):
            if backward:
                out[side, pl.ds(row, SUB)] = base[side, pl.ds(row, SUB)] - value
            else:
                out[side, pl.ds(row, SUB)] = value

        copies[0].wait()
        copies[1].wait()
        block_product([(cross_v.at[k], gathered.at[k]) for k in range(2)], sides, middle)
        copies[2].wait()
        block_product([(diag_v, total)], sides, last)

    @pl.when(flags[0] == 0)
    def _():
        out[...] = held[...]


def run_interface_step(flags, index, base, arrived, held, cross, diag, backward):
    sides, size, count = base.shape
    return pl.pallas_call(
        functools.partial(interface_step, backward=backward),
        out_shape=jax.ShapeDtypeStruct(base.shape, F32),
        in_specs=[SMEM, VMEM, VMEM, VMEM, VMEM, VMEM, VMEM, ANY, ANY],
        out_specs=VMEM,
        scratch_shapes=[
            pltpu.VMEM((2,) + diag.shape[1:], diag.dtype),
            pltpu.VMEM(diag.shape[1:], diag.dtype),
            pltpu.VMEM((2, sides, size, count), F32),
            pltpu.VMEM((sides, size, count), F32),
            pltpu.SemaphoreType.DMA((3,)),
        ],
        name="interface_backward" if backward else "interface_forward",
    )(flags, index, base, *arrived, held, cross, diag)


def interior_backward(first, flag, z, swept, diag, upper, index, *refs):
    out, diag_v, upper_v, gathered, total, result, sem, out_sem = refs[-8:]
    sides = swept.shape[0]
    levels = diag.shape[0]

    @pl.when(flag[0] != 0)
    def _():
        diag_copy = [pltpu.make_async_copy(diag.at[n], diag_v.at[n], sem.at[n]) for n in range(levels - 1)]
        upper_copy = [
            pltpu.make_async_copy(upper.at[n], upper_v.at[n], sem.at[levels - 1 + n]) for n in range(levels - 1)
        ]
        outs = []
        for n in range(levels - 2, -1, -1):
            upper_copy[n].start()
            diag_copy[n].start()

        def write(n, source):
            outs.append(pltpu.make_async_copy(source, out.at[n, pl.ds(first, sides)], out_sem.at[n]))
            outs[-1].start()

        write(levels - 1, swept)
        for n in range(levels - 2, -1, -1):
            source = swept if n == levels - 2 else result.at[n + 1]
            upper_copy[n].wait()
            for k in range(2):
                take_blocks(gathered.at[k], source, index[n, k][None])

            def middle(side, row, value):
                total[side, pl.ds(row, SUB)] = value

            def last(side, row, value, n=n):
                result[n, side, pl.ds(row, SUB)] = z[n, side, pl.ds(row, SUB)] - value

            block_product([(upper_v.at[n, k], gathered.at[k]) for k in range(2)], sides, middle)
            diag_copy[n].wait()
            block_product([(diag_v.at[n], total)], sides, last)
            write(n, result.at[n])
        for copy in outs:
            copy.wait()


def run_interior_backward(first, flag, z, swept, diag, upper, index, all_sides, earlier):
    sides, size, count = swept.shape
    levels = diag.shape[0]
    return pl.pallas_call(
        functools.partial(interior_backward, first),
        out_shape=jax.ShapeDtypeStruct((levels, all_sides, size, count), F32),
        in_specs=[SMEM, VMEM, VMEM, ANY, ANY, VMEM] + ([] if earlier is None else [ANY]),
        out_specs=ANY,
        input_output_aliases={} if earlier is None else {6: 0},
        scratch_shapes=[
            pltpu.VMEM((levels - 1,) + diag.shape[1:], diag.dtype),
            pltpu.VMEM(upper.shape, upper.dtype),
            pltpu.VMEM((2, sides, size, count), F32),
            pltpu.VMEM((sides, size, count), F32),
            pltpu.VMEM((levels - 1, sides, size, count), F32),
            pltpu.SemaphoreType.DMA((2 * levels - 2,)),
            pltpu.SemaphoreType.DMA((levels,)),
        ],
        name="interior_backward",
    )(flag, z, swept, diag, upper, index, *(() if earlier is None else (earlier,)))


def hop_pairs(strips, doms, sender, receiver):
    def flat(s, p):
        return s * doms + p

    odd = [
        (flat(sender, p), flat(receiver, q))
        for i in range(1, doms - 1, 2)
        for p, q in ((i, i + 1), (i + 1, i))
    ]
    turn = sender ^ receiver
    if strips & (strips - 1) == 0 and doms % 2 == 0:
        every = [(s, p) for s in range(strips) for p in range(doms)]
        even = [(flat(s, p), flat(s ^ turn, p ^ 1)) for s, p in every]
        straight = [(flat(s, p), flat(s ^ turn, p)) for s, p in every]
    else:
        even = [(flat(sender, p), flat(receiver, p ^ 1)) for p in range(doms) if p ^ 1 < doms]
        straight = [(flat(sender, p), flat(receiver, p)) for p in range(doms)]
    return odd, even, straight


def on_device(rhs, diag, lower, lower_index, upper, upper_index, cross_low, cross_low_index, cross_up, cross_up_index):
    strips, doms = lax.axis_size("strip"), lax.axis_size("dom")
    strip, dom = lax.axis_index("strip"), lax.axis_index("dom")
    all_sides = rhs.shape[1]
    sides = all_sides // WAVES
    parity = dom % 2

    def flag(condition):
        return jnp.reshape(condition.astype(jnp.int32), (1,))

    on = jnp.ones((1,), jnp.int32)
    first_strip = flag(strip == 0)

    def forward(wave, which):
        return run_interior_forward(wave * sides, which, rhs, diag, lower, lower_index, sides)

    def hop(state, base, sender, receiver, cross, cross_index, backward):
        odd, even, straight = hop_pairs(strips, doms, sender, receiver)

        def go(state, base):
            axes = ("strip", "dom")
            from_odd = lax.ppermute(state, axes, odd)
            from_even = lax.ppermute(state, axes, even)
            own = lax.ppermute(state, axes, straight)
            flags = jnp.stack([(strip == receiver).astype(jnp.int32), parity])
            return run_interface_step(
                flags, cross_index, base, (own, from_even, from_odd), state, cross, diag, backward
            )

        return lax.cond((strip == sender) | (strip == receiver), go, lambda state, base: state, state, base)

    parts = [forward(wave, on) for wave in range(WAVES)]
    z = [p[0] for p in parts]
    local = [p[1] for p in parts]
    state = [p[2] for p in parts]
    interface = [None] * WAVES
    hops = strips - 1
    for turn in range(2 * hops + SPACING * (WAVES - 1)):
        for wave in range(WAVES):
            slot = turn - SPACING * wave
            if 0 <= slot < hops:
                state[wave] = hop(
                    state[wave], local[wave], slot, slot + 1, cross_low, cross_low_index, False
                )
            elif hops <= slot < 2 * hops:
                if slot == hops:
                    interface[wave] = state[wave]
                sender = 2 * hops - slot
                state[wave] = hop(
                    state[wave], interface[wave], sender, sender - 1, cross_up, cross_up_index, True
                )
            if WAVES > 1:
                state = list(lax.optimization_barrier(tuple(state)))
    out = None
    for wave in range(WAVES):
        out = run_interior_backward(
            wave * sides, on, z[wave], state[wave], diag, upper, upper_index, all_sides, out
        )
    return out


def solution(mesh):
    wide = P("strip", None, None, "dom")
    blocks = P("strip", None, None, None, "dom")
    index = P("strip", None, "dom")
    in_specs = (wide, wide, blocks, index, blocks, index, blocks, index, blocks, index)
    return jax.shard_map(on_device, mesh=mesh, in_specs=in_specs, out_specs=wide, check_vma=False)
```

time: 876 us -> 260 us (0.30)
  the two profiles are of different devices: /device:TPU:27 before, /device:TPU:0 now
where the time goes in v1:
time: 260 us
  starting transfers between devices  189 us (73%)
  Pallas kernels  56.3 us (22%)
  waiting for transfers between devices  7.03 us (3%)
  local copies, waits for them, and re-layouts  3.41 us (1%)
    ppermute x4, starting transfers between devices, go(): from_even = lax.ppermute(state, axes, even)  182 us
    pallas_call x2, Pallas kernels, run_interior_forward(): pl.pallas_call(functools.partial(interior_forward, first), out_shape=[jax...  22.2 us
    pallas_call x2, Pallas kernels, run_interior_backward(): pl.pallas_call(functools.partial(interior_backward, first), out_shape=jax...  21.7 us
    pallas_call x4, Pallas kernels, run_interface_step(): pl.pallas_call(functools.partial(interface_step, backward=backward), out_...  12.5 us
    ppermute x4, waiting for transfers between devices, go(): from_even = lax.ppermute(state, axes, even)  6.29 us
  transfers between devices with their start and end apart: 12, of which 4 were waited for; matrix products, arithmetic and copies ran while one was open for 1% of the time, Pallas kernels for 0%

profile of v1, /device:TPU:0, one launch (start us, length us, event | category | flops | bytes accessed | tf_op | source)
XLA Modules:
  0.0 259.8 jit_solution(13074857823789201939)
XLA Ops:
  0.0 11.2 %interior_forward.3 = (f32[3,4,64,128]{3,2,1,0:T(8,128)}, f32[4,64,128]{2,1,0:T(8,128)S(1)}, f32[4,64,128]{2,1,0:T(8,128)S(1)}) custom-call(s32[1]{0:T(128)} %constant.68.clone.1.flag, f32[4,8,64,128]{3,2,1,0:T(8,128)} %rhs.3, bf16[4,64,64,128]{3,2,1,0:T(8,128)(2,1)} %diag.7, bf16[3,2,64,64,128]{4,3,2,1,0:T(8,128)(2,1)} %lower.3, s32[3,2,128]{2,1,0:T(2,128)} %index.5), custom_call_target="tpu_custom_call" | custom-call | tf_op jit(solution)/shard_map/interior_forward/pallas_call | solution.py:128
  11.2 9.0 %conditional.28 = (f32[4,64,128]{2,1,0:T(8,128)S(1)}) conditional(s32[]{:T(128)} %convert_element_type.21, f32[4,64,128]{2,1,0:T(8,128)S(1)} %get-tuple-element.762, (s32[]{:T(128)}, s32[]{:T(128)}, f32[4,64,128]{2,1,0:T(8,128)S(1)}, s32[1,2,128]{2,1,0:T(2,128)S(1)}, f32[4,64,128]{2,1,0:T(8,128)S(1)}, ...), branch_computations={%region_0.1_spmd, %region_1.2_spmd} | conditional | flops 4 | bytes 3932430 | solution.py:309
  11.2 0.7 collective-permute-start.2
  11.9 3.2 %collective-permute-start.1 = (f32[4,64,128]{2,1,0:T(8,128)S(1)}, f32[4,64,128]{2,1,0:T(8,128)S(1)}, u32[]{:S(2)}, u32[]{:S(2)}) collective-permute-start(f32[4,64,128]{2,1,0:T(8,128)S(1)} %copy.69.held), channel_id=1, source_target_pairs={{0,5},{1,4},{2,7},{3,6},{4,1},{5,0},{6,3},{7,2},{8,13},{9,12},{10,... | collective-permute-start | bytes 393224 | tf_op jit(solution)/shard_map/cond/branch_1_fun/ppermute | solution.py:302
  15.1 2.3 collective-permute-start
  17.4 0.7 pad_add_fusion.flags
  18.1 0.3 collective-permute-done.straight
  18.4 0.3 copy-done.29
  18.7 0.0 copy-done.57
  18.8 0.3 copy-done.85
  19.1 1.1 interface_forward.14
  20.2 11.0 %interior_forward.2 = (f32[3,4,64,128]{3,2,1,0:T(8,128)}, f32[4,64,128]{2,1,0:T(8,128)S(1)}, f32[4,64,128]{2,1,0:T(8,128)S(1)}) custom-call(s32[1]{0:T(128)} %constant.68.clone.1.flag, f32[4,8,64,128]{3,2,1,0:T(8,128)} %rhs.3, bf16[4,64,64,128]{3,2,1,0:T(8,128)(2,1)} %diag.7, bf16[3,2,64,64,128]{4,3,2,1,0:T(8,128)(2,1)} %lower.3, s32[3,2,128]{2,1,0:T(2,128)} %index.5), custom_call_target="tpu_custom_call" | custom-call | tf_op jit(solution)/shard_map/interior_forward/pallas_call | solution.py:128
  31.3 20.7 %conditional.31 = (f32[4,64,128]{2,1,0:T(8,128)S(1)}) conditional(s32[]{:T(128)} %convert_element_type.21, f32[4,64,128]{2,1,0:T(8,128)S(1)} %get-tuple-element.770, (s32[]{:T(128)}, s32[]{:T(128)}, f32[4,64,128]{2,1,0:T(8,128)S(1)}, s32[1,2,128]{2,1,0:T(2,128)S(1)}, f32[4,64,128]{2,1,0:T(8,128)S(1)}, ...), branch_computations={%region_6.7_spmd, %region_7.8_spmd} | conditional | flops 4 | bytes 3932430 | solution.py:309
  31.3 0.7 collective-permute-start.11
  32.0 14.6 %collective-permute-start.10 = (f32[4,64,128]{2,1,0:T(8,128)S(1)}, f32[4,64,128]{2,1,0:T(8,128)S(1)}, u32[]{:S(2)}, u32[]{:S(2)}) collective-permute-start(f32[4,64,128]{2,1,0:T(8,128)S(1)} %copy.72.held), channel_id=1, source_target_pairs={{0,5},{1,4},{2,7},{3,6},{4,1},{5,0},{6,3},{7,2},{8,13},{9,12},{10,... | collective-permute-start | bytes 393224 | tf_op jit(solution)/shard_map/cond/branch_1_fun/ppermute | solution.py:302
  46.6 2.6 %collective-permute-start.9 = (f32[4,64,128]{2,1,0:T(8,128)S(1)}, f32[4,64,128]{2,1,0:T(8,128)S(1)}, u32[]{:S(2)}, u32[]{:S(2)}) collective-permute-start(f32[4,64,128]{2,1,0:T(8,128)S(1)} %copy.72.held), channel_id=1, source_target_pairs={{0,4},{1,5},{2,6},{3,7},{4,0},{5,1},{6,2},{7,3},{8,12},{9,13},{10,... | collective-permute-start | bytes 393224 | tf_op jit(solution)/shard_map/cond/branch_1_fun/ppermute | solution.py:303
  49.2 0.6 pad_add_fusion.3.flags
  49.7 0.0 collective-permute-done.11.odd
  49.8 0.0 collective-permute-done.10.pair
  49.8 0.4 collective-permute-done.9.straight
  50.2 0.2 copy-done.32
  50.4 0.1 copy-done.60
  50.5 0.3 copy-done.88
  50.8 1.1 interface_forward.17
  52.1 0.2 conditional.38
  52.3 0.0 copy-start.28
  52.3 0.7 copy-done.28
  53.2 154.3 %conditional.52 = (f32[4,64,128]{2,1,0:T(8,128)S(1)}) conditional(s32[]{:T(128)} %convert_element_type.21, f32[4,64,128]{2,1,0:T(8,128)S(1)} %get-tuple-element.845, (s32[]{:T(128)}, s32[]{:T(128)}, f32[4,64,128]{2,1,0:T(8,128)S(1)}, s32[1,2,128]{2,1,0:T(2,128)S(1)}, f32[4,64,128]{2,1,0:T(8,128)S(1)}, ...), branch_computations={%region_48.49_spmd, %region_49.50_spmd} | conditional | flops 4 | bytes 3932430 | solution.py:309
  53.3 0.7 collective-permute-start.74
  53.9 144.1 %collective-permute-start.73 = (f32[4,64,128]{2,1,0:T(8,128)S(1)}, f32[4,64,128]{2,1,0:T(8,128)S(1)}, u32[]{:S(2)}, u32[]{:S(2)}) collective-permute-start(f32[4,64,128]{2,1,0:T(8,128)S(1)} %copy.91.held), channel_id=1, source_target_pairs={{0,5},{1,4},{2,7},{3,6},{4,1},{5,0},{6,3},{7,2},{8,13},{9,12},{10,... | collective-permute-start | bytes 393224 | tf_op jit(solution)/shard_map/cond/branch_1_fun/ppermute | solution.py:302
  198.0 0.0 collective-permute-start.72
  198.0 0.7 pad_add_fusion.24.flags
  198.7 3.1 %collective-permute-done.73.pair = f32[4,64,128]{2,1,0:T(8,128)S(1)} collective-permute-done((f32[4,64,128]{2,1,0:T(8,128)S(1)}, f32[4,64,128]{2,1,0:T(8,128)S(1)}, u32[]{:S(2)}, u32[]{:S(2)}) %collective-permute-start.73) | collective-permute-done | bytes 131104 | tf_op jit(solution)/shard_map/cond/branch_1_fun/ppermute | solution.py:302
  201.8 0.0 collective-permute-done.72.straight
  201.8 0.6 copy-done.79
  202.5 0.0 copy-done.107
  202.5 5.1 %interface_backward.24 = f32[4,64,128]{2,1,0:T(8,128)S(1)} custom-call(s32[2]{0:T(128)} %pad_add_fusion.24.flags, s32[1,2,128]{2,1,0:T(2,128)S(1)} %get-tuple-element.673.index, f32[4,64,128]{2,1,0:T(8,128)S(1)} %get-tuple-element.674.base, f32[4,64,128]{2,1,0:T(8,128)} %copy-done.107, f32[4,64,128]{2,1,0:T(8,128)} %copy-done.79, f32[4,64,128]{2,1,0:T(8,128)} %copy-done.51, ...), custom_call_target="tpu_custom_call" | custom-call | tf_op jit(solution)/shard_map/cond/branch_1_fun/interface_backward/pallas_call | solution.py:181
  207.6 0.2 conditional.53
  207.8 30.1 %conditional.55 = (f32[4,64,128]{2,1,0:T(8,128)S(1)}) conditional(s32[]{:T(128)} %convert_element_type.21, f32[4,64,128]{2,1,0:T(8,128)S(1)} %get-tuple-element.849, (s32[]{:T(128)}, s32[]{:T(128)}, f32[4,64,128]{2,1,0:T(8,128)S(1)}, s32[1,2,128]{2,1,0:T(2,128)S(1)}, f32[4,64,128]{2,1,0:T(8,128)S(1)}, ...), branch_computations={%region_54.55_spmd, %region_55.56_spmd} | conditional | flops 4 | bytes 3932430 | solution.py:309
  207.9 0.7 collective-permute-start.83
  208.5 19.8 %collective-permute-start.82 = (f32[4,64,128]{2,1,0:T(8,128)S(1)}, f32[4,64,128]{2,1,0:T(8,128)S(1)}, u32[]{:S(2)}, u32[]{:S(2)}) collective-permute-start(f32[4,64,128]{2,1,0:T(8,128)S(1)} %copy.94.held), channel_id=1, source_target_pairs={{0,5},{1,4},{2,7},{3,6},{4,1},{5,0},{6,3},{7,2},{8,13},{9,12},{10,... | collective-permute-start | bytes 393224 | tf_op jit(solution)/shard_map/cond/branch_1_fun/ppermute | solution.py:302
  228.4 0.6 pad_add_fusion.27.flags
  229.0 3.2 %collective-permute-done.82.pair = f32[4,64,128]{2,1,0:T(8,128)S(1)} collective-permute-done((f32[4,64,128]{2,1,0:T(8,128)S(1)}, f32[4,64,128]{2,1,0:T(8,128)S(1)}, u32[]{:S(2)}, u32[]{:S(2)}) %collective-permute-start.82) | collective-permute-done | bytes 131104 | tf_op jit(solution)/shard_map/cond/branch_1_fun/ppermute | solution.py:302
  232.2 0.6 copy-done.82
  232.8 0.0 copy-done.110
  232.8 5.1 %interface_backward.27 = f32[4,64,128]{2,1,0:T(8,128)S(1)} custom-call(s32[2]{0:T(128)} %pad_add_fusion.27.flags, s32[1,2,128]{2,1,0:T(2,128)S(1)} %get-tuple-element.694.index, f32[4,64,128]{2,1,0:T(8,128)S(1)} %get-tuple-element.695.base, f32[4,64,128]{2,1,0:T(8,128)} %copy-done.110, f32[4,64,128]{2,1,0:T(8,128)} %copy-done.82, f32[4,64,128]{2,1,0:T(8,128)} %copy-done.54, ...), custom_call_target="tpu_custom_call" | custom-call | tf_op jit(solution)/shard_map/cond/branch_1_fun/interface_backward/pallas_call | solution.py:181
  237.9 10.9 %interior_backward.2.refs_0_ = f32[4,8,64,128]{3,2,1,0:T(8,128)} custom-call(s32[1]{0:T(128)} %constant.68.clone.1.flag, f32[3,4,64,128]{3,2,1,0:T(8,128)} %get-tuple-element.821.z, f32[4,64,128]{2,1,0:T(8,128)S(1)} %get-tuple-element.847.swept, bf16[4,64,64,128]{3,2,1,0:T(8,128)(2,1)} %diag.7, bf16[3,2,64,64,128]{4,3,2,1,0:T(8,128)(2,1)} %upper.3, ...), custom_call_target="tpu_custom_call" | custom-call | tf_op jit(solution)/shard_map/interior_backward/pallas_call | solution.py:241
  248.8 10.9 %interior_backward.3 = f32[4,8,64,128]{3,2,1,0:T(8,128)} custom-call(s32[1]{0:T(128)} %constant.68.clone.1.flag, f32[3,4,64,128]{3,2,1,0:T(8,128)} %get-tuple-element.761.z, f32[4,64,128]{2,1,0:T(8,128)S(1)} %get-tuple-element.850.swept, bf16[4,64,64,128]{3,2,1,0:T(8,128)(2,1)} %diag.7, ...), custom_call_target="tpu_custom_call", output_to_operand_aliasing={{}: (6, {})} | custom-call | tf_op jit(solution)/shard_map/interior_backward/pallas_call | solution.py:241
  (60 shorter events, 0.4 us)
Async XLA Ops:
  0.0 11.2 %copy-start = (bf16[1,2,64,64,128]{4,3,2,1,0:T(8,128)(2,1)S(1)}, bf16[1,2,64,64,128]{4,3,2,1,0:T(8,128)(2,1)}, u32[]{:S(2)}) copy-start(bf16[1,2,64,64,128]{4,3,2,1,0:T(8,128)(2,1)} %param.72) | copy-start | bytes 6291460
  0.0 11.2 %copy-start.27 = (s32[1,2,128]{2,1,0:T(2,128)S(1)}, s32[1,2,128]{2,1,0:T(2,128)}, u32[]{:S(2)}) copy-start(s32[1,2,128]{2,1,0:T(2,128)} %param.73) | copy-start | bytes 3076
  11.2 7.2 %copy-start.1 = (f32[4,64,128]{2,1,0:T(8,128)}, f32[4,64,128]{2,1,0:T(8,128)S(1)}, u32[]{:S(2)}) copy-start(f32[4,64,128]{2,1,0:T(8,128)S(1)} %copy.69.held) | copy-start | bytes 393220 | tf_op jit(solution)/shard_map/cond
  11.2 6.8 %collective-permute-start.2 = (f32[4,64,128]{2,1,0:T(8,128)S(1)}, f32[4,64,128]{2,1,0:T(8,128)S(1)}, u32[]{:S(2)}, u32[]{:S(2)}) collective-permute-start(f32[4,64,128]{2,1,0:T(8,128)S(1)} %copy.69.held), channel_id=1, source_target_pairs={{1,6},{2,5}} | collective-permute-start | bytes 393224 | tf_op jit(solution)/shard_map/cond/branch_1_fun/ppermute | solution.py:301
  11.9 6.2 %collective-permute-start.1 = (f32[4,64,128]{2,1,0:T(8,128)S(1)}, f32[4,64,128]{2,1,0:T(8,128)S(1)}, u32[]{:S(2)}, u32[]{:S(2)}) collective-permute-start(f32[4,64,128]{2,1,0:T(8,128)S(1)} %copy.69.held), channel_id=1, source_target_pairs={{0,5},{1,4},{2,7},{3,6},{4,1},{5,0},{6,3},{7,2},{8,13},{9,12},{10,... | collective-permute-start | bytes 393224 | tf_op jit(solution)/shard_map/cond/branch_1_fun/ppermute | solution.py:302
  15.1 3.3 %collective-permute-start = (f32[4,64,128]{2,1,0:T(8,128)S(1)}, f32[4,64,128]{2,1,0:T(8,128)S(1)}, u32[]{:S(2)}, u32[]{:S(2)}) collective-permute-start(f32[4,64,128]{2,1,0:T(8,128)S(1)} %copy.69.held), channel_id=1, source_target_pairs={{0,4},{1,5},{2,6},{3,7},{4,0},{5,1},{6,2},{7,3},{8,12},{9,13},{10,... | collective-permute-start | bytes 393224 | tf_op jit(solution)/shard_map/cond/branch_1_fun/ppermute | solution.py:303
  18.1 0.7 copy-start.29
  18.1 0.7 copy-start.57
  18.4 0.7 copy-start.85
  31.3 18.9 %copy-start.4 = (f32[4,64,128]{2,1,0:T(8,128)}, f32[4,64,128]{2,1,0:T(8,128)S(1)}, u32[]{:S(2)}) copy-start(f32[4,64,128]{2,1,0:T(8,128)S(1)} %copy.72.held) | copy-start | bytes 393220 | tf_op jit(solution)/shard_map/cond
  31.3 18.4 %collective-permute-start.11 = (f32[4,64,128]{2,1,0:T(8,128)S(1)}, f32[4,64,128]{2,1,0:T(8,128)S(1)}, u32[]{:S(2)}, u32[]{:S(2)}) collective-permute-start(f32[4,64,128]{2,1,0:T(8,128)S(1)} %copy.72.held), channel_id=1, source_target_pairs={{1,6},{2,5}} | collective-permute-start | bytes 393224 | tf_op jit(solution)/shard_map/cond/branch_1_fun/ppermute | solution.py:301
  32.0 17.8 %collective-permute-start.10 = (f32[4,64,128]{2,1,0:T(8,128)S(1)}, f32[4,64,128]{2,1,0:T(8,128)S(1)}, u32[]{:S(2)}, u32[]{:S(2)}) collective-permute-start(f32[4,64,128]{2,1,0:T(8,128)S(1)} %copy.72.held), channel_id=1, source_target_pairs={{0,5},{1,4},{2,7},{3,6},{4,1},{5,0},{6,3},{7,2},{8,13},{9,12},{10,... | collective-permute-start | bytes 393224 | tf_op jit(solution)/shard_map/cond/branch_1_fun/ppermute | solution.py:302
  46.6 3.6 %collective-permute-start.9 = (f32[4,64,128]{2,1,0:T(8,128)S(1)}, f32[4,64,128]{2,1,0:T(8,128)S(1)}, u32[]{:S(2)}, u32[]{:S(2)}) collective-permute-start(f32[4,64,128]{2,1,0:T(8,128)S(1)} %copy.72.held), channel_id=1, source_target_pairs={{0,4},{1,5},{2,6},{3,7},{4,0},{5,1},{6,2},{7,3},{8,12},{9,13},{10,... | collective-permute-start | bytes 393224 | tf_op jit(solution)/shard_map/cond/branch_1_fun/ppermute | solution.py:303
  49.8 0.7 copy-start.32
  49.8 0.7 copy-start.60
  50.2 0.7 copy-start.88
  52.3 0.7 copy-start.28
  53.3 148.5 %copy-start.23 = (f32[4,64,128]{2,1,0:T(8,128)}, f32[4,64,128]{2,1,0:T(8,128)S(1)}, u32[]{:S(2)}) copy-start(f32[4,64,128]{2,1,0:T(8,128)S(1)} %copy.91.held) | copy-start | bytes 393220 | tf_op jit(solution)/shard_map/cond
  53.3 145.4 %collective-permute-start.74 = (f32[4,64,128]{2,1,0:T(8,128)S(1)}, f32[4,64,128]{2,1,0:T(8,128)S(1)}, u32[]{:S(2)}, u32[]{:S(2)}) collective-permute-start(f32[4,64,128]{2,1,0:T(8,128)S(1)} %copy.91.held), channel_id=1, source_target_pairs={{5,2},{6,1}} | collective-permute-start | bytes 393224 | tf_op jit(solution)/shard_map/cond/branch_1_fun/ppermute | solution.py:301
  53.9 147.8 %collective-permute-start.73 = (f32[4,64,128]{2,1,0:T(8,128)S(1)}, f32[4,64,128]{2,1,0:T(8,128)S(1)}, u32[]{:S(2)}, u32[]{:S(2)}) collective-permute-start(f32[4,64,128]{2,1,0:T(8,128)S(1)} %copy.91.held), channel_id=1, source_target_pairs={{0,5},{1,4},{2,7},{3,6},{4,1},{5,0},{6,3},{7,2},{8,13},{9,12},{10,... | collective-permute-start | bytes 393224 | tf_op jit(solution)/shard_map/cond/branch_1_fun/ppermute | solution.py:302
  198.0 3.8 %collective-permute-start.72 = (f32[4,64,128]{2,1,0:T(8,128)S(1)}, f32[4,64,128]{2,1,0:T(8,128)S(1)}, u32[]{:S(2)}, u32[]{:S(2)}) collective-permute-start(f32[4,64,128]{2,1,0:T(8,128)S(1)} %copy.91.held), channel_id=1, source_target_pairs={{0,4},{1,5},{2,6},{3,7},{4,0},{5,1},{6,2},{7,3},{8,12},{9,13},{10,... | collective-permute-start | bytes 393224 | tf_op jit(solution)/shard_map/cond/branch_1_fun/ppermute | solution.py:303
  198.7 3.1 %copy-start.51 = (f32[4,64,128]{2,1,0:T(8,128)}, f32[4,64,128]{2,1,0:T(8,128)S(1)}, u32[]{:S(2)}) copy-start(f32[4,64,128]{2,1,0:T(8,128)S(1)} %collective-permute-done.74.odd) | copy-start | bytes 393220 | tf_op jit(solution)/shard_map/cond
  201.8 0.7 copy-start.79
  201.8 0.7 copy-start.107
  207.9 24.3 %copy-start.26 = (f32[4,64,128]{2,1,0:T(8,128)}, f32[4,64,128]{2,1,0:T(8,128)S(1)}, u32[]{:S(2)}) copy-start(f32[4,64,128]{2,1,0:T(8,128)S(1)} %copy.94.held) | copy-start | bytes 393220 | tf_op jit(solution)/shard_map/cond
  207.9 21.1 %collective-permute-start.83 = (f32[4,64,128]{2,1,0:T(8,128)S(1)}, f32[4,64,128]{2,1,0:T(8,128)S(1)}, u32[]{:S(2)}, u32[]{:S(2)}) collective-permute-start(f32[4,64,128]{2,1,0:T(8,128)S(1)} %copy.94.held), channel_id=1, source_target_pairs={{5,2},{6,1}} | collective-permute-start | bytes 393224 | tf_op jit(solution)/shard_map/cond/branch_1_fun/ppermute | solution.py:301
  208.5 23.6 %collective-permute-start.82 = (f32[4,64,128]{2,1,0:T(8,128)S(1)}, f32[4,64,128]{2,1,0:T(8,128)S(1)}, u32[]{:S(2)}, u32[]{:S(2)}) collective-permute-start(f32[4,64,128]{2,1,0:T(8,128)S(1)} %copy.94.held), channel_id=1, source_target_pairs={{0,5},{1,4},{2,7},{3,6},{4,1},{5,0},{6,3},{7,2},{8,13},{9,12},{10,... | collective-permute-start | bytes 393224 | tf_op jit(solution)/shard_map/cond/branch_1_fun/ppermute | solution.py:302
  228.4 3.8 %collective-permute-start.81 = (f32[4,64,128]{2,1,0:T(8,128)S(1)}, f32[4,64,128]{2,1,0:T(8,128)S(1)}, u32[]{:S(2)}, u32[]{:S(2)}) collective-permute-start(f32[4,64,128]{2,1,0:T(8,128)S(1)} %copy.94.held), channel_id=1, source_target_pairs={{0,4},{1,5},{2,6},{3,7},{4,0},{5,1},{6,2},{7,3},{8,12},{9,13},{10,... | collective-permute-start | bytes 393224 | tf_op jit(solution)/shard_map/cond/branch_1_fun/ppermute | solution.py:303
  229.0 3.2 %copy-start.54 = (f32[4,64,128]{2,1,0:T(8,128)}, f32[4,64,128]{2,1,0:T(8,128)S(1)}, u32[]{:S(2)}) copy-start(f32[4,64,128]{2,1,0:T(8,128)S(1)} %collective-permute-done.83.odd) | copy-start | bytes 393220 | tf_op jit(solution)/shard_map/cond
  232.1 0.7 copy-start.82
  232.1 0.7 copy-start.110
